TPU v7x, 256 devices: a whole 4x4x8 slice. The times are simulated.
256 devices in a mesh: lat: 8 (over x, core), lon: 32 (over z, y).
Axes of the slice: x: 4, y: 4, z: 8, core: 2. Of those that a mesh axis runs over, the one named last changes fastest.
Arguments:
- features: float32 [32, 256, 4096], P('lat', None, 'lon'), may hold values from -6 to 6
- basis_panels: float32 [32, 3, 9, 255], P('lat'), may hold values from -0.9 to 0.9
- weights: float32 [9, 256, 256], replicated, may hold values from -0.125 to 0.125
- bias_term: float32 [256], replicated, may hold values from -3 to 3
- widths: int32 [32], P('lat'), may hold values from 4 to 127, as said below
- tap_rows: int32 [32, 3], P('lat'), may hold values from -4 to 4, as said below
Outputs:
- convolved: float32 [32, 256, 4096], P('lat', None, 'lon')
Inputs may be any that keep to these rules, and one draw needn't show every extreme that they name: With d = min(i, 31 - i) the distance of row i from the nearer pole, widths[i] is at most min(8 * 32 // (4 * d + 2) + 4, 127), and the first and the last row have the half-width 127. In each aligned block of 4 rows the row nearest a pole has exactly this bound. `tap_rows`: the first row's first tap has the offset -4 and the last row's last tap the offset 4.
All inputs are finite; a program needn't handle non-finite values.
Results may differ from a plain program's by a relative error of at most 0.000062.
Values sent between devices are 32-bit elements; how exact they have to be, the bound alone decides.
A program may use at most 256 MiB of HBM per device.

v0:
```python
import jax
import jax.numpy as jnp
from jax import lax
from jax.sharding import PartitionSpec as P

REACH = 4


def passed_along(value, axis, by):
    peers = lax.axis_size(axis)
    return lax.ppermute(value, axis, [(i, (i + by) % peers) for i in range(peers)])


def padded_2(block, sides, width):
    for axis, dim in sides:
        count = lax.axis_size(axis)
        forward = [(i, i + 1) for i in range(count - 1)]
        backward = [(target, source) for source, target in forward]
        low = lax.ppermute(
            lax.slice_in_dim(block, block.shape[dim] - width, None, axis=dim), axis, forward
        )
        high = lax.ppermute(lax.slice_in_dim(block, 0, width, axis=dim), axis, backward)
        block = jnp.concatenate([low, block, high], axis=dim)
    return block


def widen(block):
    columns = block.shape[2]
    before = []
    needed = columns - 1
    before.insert(0, passed_along(block[:, :, columns - needed :], "lon", 1))
    after = [passed_along(block[:, :, :needed], "lon", -1)]
    return jnp.concatenate(before + [block] + after, axis=2)


def deepen(block, lon_count):
    padded = padded_2(block, (("lat", 0),), REACH)
    lat_place = lax.axis_index("lat")
    lat_last = lax.axis_size("lat") - 1
    outgoing = jnp.where(lat_place == 0, block, block)
    mirrored = passed_along(outgoing, "lon", lon_count // 2)[::-1]
    upper = jnp.where(lat_place == 0, mirrored, padded[:REACH])
    lower = jnp.where(lat_place == lat_last, mirrored, padded[-REACH:])
    return jnp.concatenate([upper, padded[REACH:-REACH], lower], axis=0)


def per_device(features, basis_panels, weights, bias_term, widths, tap_rows):
    row_count, channels, columns = features.shape
    lon_count = lax.axis_size("lon")
    hop_count = min(1, lon_count // 2)
    half_width = hop_count * columns - 1
    extended = deepen(widen(features), lon_count)
    window = extended.shape[2]
    lag_table = (
        jnp.arange(window, dtype=jnp.int32)[:, None] - jnp.arange(columns, dtype=jnp.int32)[None, :]
    )
    clipped = jnp.clip(lag_table, 0, 2 * half_width)
    in_panel = (lag_table >= 0) & (lag_table <= 2 * half_width)

    def one_row(row_index):
        reach_limit = widths[row_index]
        inside_band = in_panel & (jnp.abs(lag_table - half_width) <= reach_limit)
        gathered_panel = jnp.take(basis_panels[row_index], clipped, axis=2)
        toeplitz = jnp.where(inside_band[None, None], gathered_panel, jnp.zeros((), jnp.float32))
        chosen = jnp.take(extended, row_index + REACH + tap_rows[row_index], axis=0)
        correlated = jnp.einsum("tcm,tkml->kcl", chosen, toeplitz, precision=lax.Precision.HIGHEST)
        mixed = jnp.einsum("koc,kcl->ol", weights, correlated, precision=lax.Precision.HIGHEST)
        return mixed + bias_term[:, None]

    return lax.map(one_row, jnp.arange(row_count, dtype=jnp.int32))


def solution(mesh):
    return jax.shard_map(
        per_device,
        mesh=mesh,
        in_specs=(
            P("lat", None, "lon"),
            P("lat", None, None, None),
            P(),
            P(),
            P("lat"),
            P("lat", None),
        ),
        out_specs=P("lat", None, "lon"),
        check_vma=False,
    )
```

profile of v0, /device:TPU:32, one launch (start us, length us, event | category | flops | bytes accessed | tf_op | source)
XLA Modules:
  0.0 1406.6 jit_solution(2446659034858565069)
XLA Ops:
  0.0 1.3 copy.15
  1.4 2.6 collective-permute-start.1
  4.1 11.1 collective-permute-done.1
  15.2 4.3 collective-permute-done
  19.5 1.5 pad_maximum_fusion.1
  21.0 7.2 collective-permute-start.2
  28.2 2.4 collective-permute-start.3
  30.6 1.3 collective-permute-start.4
  31.9 63.3 %collective-permute-done.2 = f32[4,256,382]{1,0,2:T(4,128)} collective-permute-done((f32[4,256,382]{1,0,2:T(4,128)}, f32[4,256,382]{1,0,2:T(4,128)}, u32[]{:S(2)}, u32[]{:S(2)}) %collective-permute-start.2) | collective-permute-done | bytes 1564704 | tf_op jit(solution)/shard_map/ppermute | solution.py:11
  95.2 4.7 rev.3
  99.9 1.7 broadcast_select_fusion.1
  101.6 3.4 pad_maximum_fusion
  105.0 6.5 copy.19
  112.1 1294.5 %while.14 = (s32[]{:T(128)}, f32[4,256,128]{2,1,0:T(8,128)}, s32[4]{0:T(128)}, s32[4]{0:T(128)S(1)}, f32[4,3,9,255]{3,0,2,1:T(4,128)}, /*index=5*/s32[4,3]{1,0:T...) while((s32[]{:T(128)}, f32[4,256,128]{2,1,0:T(8,128)}, ...), condition=%wide.region_1.2_spmd.clone.clone, body=%wide.region_0.1_spmd.clone.clone.sunk | while | flops 4965594112 | bytes 36392804 | solution.py:70
  112.2 1.3 dynamic_slice.49
  115.4 0.9 constant_dynamic-slice_fusion.3
  116.7 244.3 %gather_fusion = f32[48896,3,9]{2,1,0:T(4,128)} fusion(f32[3,9,255]{1,0,2:T(4,128)S(1)} %bitcast.77, s32[49152]{0:T(1024)S(1)} %pad_clamp_fusion.4), kind=kCustom, calls=%fused_computation.clone.clone.1 | custom fusion | bytes 10757120 | tf_op jit(solution)/shard_map/while/body/eval_jaxpr/jit(_take)/gather | solution.py:63
  361.0 55.2 %copy.32 = f32[382,128,3,9]{1,0,2,3:T(8,128)} copy(f32[382,128,3,9]{3,2,1,0:T(4,128)} %bitcast.75) | data formatting | bytes 10561536 | tf_op jit(solution)/shard_map/while/body/eval_jaxpr/jit(_take)/gather | solution.py:63
  416.8 1.4 fusion.56
  418.3 3.0 gather_fusion.1
  421.3 11.3 fusion.58
  432.6 2.5 fusion.59
  435.2 0.7 constant_dynamic-update-slice_fusion.2
  435.8 1.3 dynamic_slice.49
  439.0 0.9 constant_dynamic-slice_fusion.3
  440.3 244.3 %gather_fusion = f32[48896,3,9]{2,1,0:T(4,128)} fusion(f32[3,9,255]{1,0,2:T(4,128)S(1)} %bitcast.77, s32[49152]{0:T(1024)S(1)} %pad_clamp_fusion.4), kind=kCustom, calls=%fused_computation.clone.clone.1 | custom fusion | bytes 10757120 | tf_op jit(solution)/shard_map/while/body/eval_jaxpr/jit(_take)/gather | solution.py:63
  684.6 55.2 %copy.32 = f32[382,128,3,9]{1,0,2,3:T(8,128)} copy(f32[382,128,3,9]{3,2,1,0:T(4,128)} %bitcast.75) | data formatting | bytes 10561536 | tf_op jit(solution)/shard_map/while/body/eval_jaxpr/jit(_take)/gather | solution.py:63
  740.4 1.4 fusion.56
  741.9 3.0 gather_fusion.1
  744.9 11.3 fusion.58
  756.2 2.5 fusion.59
  759.4 1.3 dynamic_slice.49
  762.6 0.9 constant_dynamic-slice_fusion.3
  763.9 244.3 %gather_fusion = f32[48896,3,9]{2,1,0:T(4,128)} fusion(f32[3,9,255]{1,0,2:T(4,128)S(1)} %bitcast.77, s32[49152]{0:T(1024)S(1)} %pad_clamp_fusion.4), kind=kCustom, calls=%fused_computation.clone.clone.1 | custom fusion | bytes 10757120 | tf_op jit(solution)/shard_map/while/body/eval_jaxpr/jit(_take)/gather | solution.py:63
  1008.2 55.2 %copy.32 = f32[382,128,3,9]{1,0,2,3:T(8,128)} copy(f32[382,128,3,9]{3,2,1,0:T(4,128)} %bitcast.75) | data formatting | bytes 10561536 | tf_op jit(solution)/shard_map/while/body/eval_jaxpr/jit(_take)/gather | solution.py:63
  1064.0 1.4 fusion.56
  1065.5 3.0 gather_fusion.1
  1068.4 11.3 fusion.58
  1079.8 2.5 fusion.59
  1083.0 1.3 dynamic_slice.49
  1086.2 0.9 constant_dynamic-slice_fusion.3
  1087.5 244.3 %gather_fusion = f32[48896,3,9]{2,1,0:T(4,128)} fusion(f32[3,9,255]{1,0,2:T(4,128)S(1)} %bitcast.77, s32[49152]{0:T(1024)S(1)} %pad_clamp_fusion.4), kind=kCustom, calls=%fused_computation.clone.clone.1 | custom fusion | bytes 10757120 | tf_op jit(solution)/shard_map/while/body/eval_jaxpr/jit(_take)/gather | solution.py:63
  1331.7 55.2 %copy.32 = f32[382,128,3,9]{1,0,2,3:T(8,128)} copy(f32[382,128,3,9]{3,2,1,0:T(4,128)} %bitcast.75) | data formatting | bytes 10561536 | tf_op jit(solution)/shard_map/while/body/eval_jaxpr/jit(_take)/gather | solution.py:63
  1387.6 1.4 fusion.56
  1389.0 3.0 gather_fusion.1
  1392.0 11.3 fusion.58
  1403.3 2.5 fusion.59
  1405.9 0.7 constant_dynamic-update-slice_fusion.2
  (48 shorter events, 6.5 us)
Async XLA Ops:
  1.4 13.7 collective-permute-start.1
  4.1 15.4 %collective-permute-start = (f32[4,256,127]{1,0,2:T(4,128)S(1)}, f32[4,256,127]{1,0,2:T(4,128)S(1)}, u32[]{:S(2)}, u32[]{:S(2)}) collective-permute-start(f32[4,256,127]{1,0,2:T(4,128)S(1)} %get-tuple-element.248), channel_id=1, source_target_pairs={{0,1},{1,2},{2,3},{3,4},{4,5},{5,6},{6,7},{7,8},{8,9},{9,10},{10,1... | collective-permute-start | bytes 1560584 | tf_op jit(solution)/shard_map/ppermute | solution.py:11
  21.0 74.2 %collective-permute-start.2 = (f32[4,256,382]{1,0,2:T(4,128)}, f32[4,256,382]{1,0,2:T(4,128)}, u32[]{:S(2)}, u32[]{:S(2)}) collective-permute-start(f32[4,256,382]{1,0,2:T(4,128)} %pad_maximum_fusion.1), channel_id=1, source_target_pairs={{0,16},{1,17},{2,18},{3,19},{4,20},{5,21},{6,22},{7,23},{8,24},{9,... | collective-permute-start | bytes 4694024 | tf_op jit(solution)/shard_map/ppermute | solution.py:11
  28.2 71.7 %collective-permute-start.3 = (f32[4,256,382]{1,0,2:T(4,128)}, f32[4,256,382]{1,0,2:T(4,128)}, u32[]{:S(2)}, u32[]{:S(2)}) collective-permute-start(f32[4,256,382]{1,0,2:T(4,128)} %pad_maximum_fusion.1), channel_id=1, source_target_pairs={{0,32},{32,64},{64,96},{96,128},{128,160},{160,192},{192,224},{1,3... | collective-permute-start | bytes 4694024 | tf_op jit(solution)/shard_map/ppermute | solution.py:19
  30.6 69.3 %collective-permute-start.4 = (f32[4,256,382]{1,0,2:T(4,128)}, f32[4,256,382]{1,0,2:T(4,128)}, u32[]{:S(2)}, u32[]{:S(2)}) collective-permute-start(f32[4,256,382]{1,0,2:T(4,128)} %pad_maximum_fusion.1), channel_id=1, source_target_pairs={{32,0},{64,32},{96,64},{128,96},{160,128},{192,160},{224,192},{33,... | collective-permute-start | bytes 4694024 | tf_op jit(solution)/shard_map/ppermute | solution.py:22
  105.0 7.1 copy-start
  105.0 7.1 copy-start.1
  105.0 7.1 copy-start.2
  105.0 7.1 copy-start.3
where the time goes:
time: 1420 us; the launch traced here: 1410 us
  local copies, waits for them, and re-layouts  1240 us (87%)
  waiting for transfers between devices  78.7 us (6%)
  matrix products  55.1 us (4%)
    gather x8, local copies, waits for them, and re-layouts, one_row(): gathered_panel = jnp.take(basis_panels[row_index], clipped, axis=2)  1200 us
    ppermute x3, waiting for transfers between devices, passed_along(): lax.ppermute(value, axis, [(i, (i + by) % peers) for i in range(peers)])  78.7 us
    dot_general x4, matrix products, one_row(): jnp.einsum('tcm,tkml->kcl', chosen, toeplitz, precision=lax.Precision.HIG...  45.2 us
  transfers between devices with their start and end apart: 5, of which 3 were waited for; matrix products, arithmetic and copies ran while one was open for 0% of the time, Pallas kernels for 0%

commit v1 on v0

v1 whole, which is shorter than its diff:
```python
import functools

import jax
import jax.numpy as jnp
from jax import lax
from jax.experimental import pallas as pl
from jax.experimental.pallas import tpu as pltpu
from jax.sharding import PartitionSpec as P

ROWS = 4
TAPS = 3
K = 9
SPAN = 255
WMAX = 127
L = 128
HALO = (128, 48, 32, 32)
BASE = (0, 128, 176, 208)
HALOS = 240
MESH = pl.DeviceIdType.MESH
NT = (((1,), (1,)), ((), ()))


def split(x):
    high = x.astype(jnp.bfloat16)
    low = (x - high.astype(jnp.float32)).astype(jnp.bfloat16)
    return high, low


def kernel(
    lats, lons,
    widths, taps, bias, basis, feat, weights,
    out,
    ext, wf, wh, wl, panel, bands, t0, t1, t2, t3, xs, ch, cl, acc, hsend, hrecv,
    send_sem, recv_sem, hsend_sem, hrecv_sem, own_sem, w_sem,
):
    la, lo = lax.axis_index("lat"), lax.axis_index("lon")
    channels = ext.shape[1]
    east = {"lat": la, "lon": lax.rem(lo + 1, lons)}
    west = {"lat": la, "lon": lax.rem(lo + lons - 1, lons)}
    half = {"lat": la, "lon": lax.rem(lo + lons // 2, lons)}
    above = {"lat": lax.rem(la + lats - 1, lats), "lon": lo}
    below = {"lat": lax.rem(la + 1, lats), "lon": lo}
    first, last = la == 0, la == lats - 1

    barrier = pltpu.get_barrier_semaphore()

    def greet(peer):
        pl.semaphore_signal(barrier, inc=1, device_id=peer, device_id_type=MESH)

    greet(east)
    greet(west)

    @pl.when(first)
    def _():
        greet(half)

    @pl.when(jnp.logical_not(first))
    def _():
        greet(above)

    @pl.when(last)
    def _():
        greet(half)

    @pl.when(jnp.logical_not(last))
    def _():
        greet(below)

    own = pltpu.make_async_copy(feat, ext.at[pl.ds(ROWS, ROWS)], own_sem)
    fetch = pltpu.make_async_copy(weights, wf, w_sem)
    own.start()
    fetch.start()
    pl.semaphore_wait(barrier, 4)

    def send(src, dst, place, peer):
        return pltpu.make_async_remote_copy(
            src_ref=feat.at[src], dst_ref=ext.at[dst], send_sem=send_sem.at[place],
            recv_sem=recv_sem.at[dst], device_id=peer, device_id_type=MESH,
        )

    @pl.when(first)
    def _():
        for r in range(ROWS):
            send(r, ROWS - 1 - r, r, half).start()

    @pl.when(last)
    def _():
        for r in range(ROWS):
            send(r, 3 * ROWS - 1 - r, ROWS + r, half).start()

    @pl.when(jnp.logical_not(first))
    def _():
        for r in range(ROWS):
            send(r, 2 * ROWS + r, r, above).start()

    @pl.when(jnp.logical_not(last))
    def _():
        for r in range(ROWS):
            send(r, r, ROWS + r, below).start()

    flip = la // (lats // 2)
    rows = [s + flip * (ROWS - 1 - 2 * s) for s in range(ROWS)]
    tables = (t0, t1, t2, t3)

    panel[...] = jnp.zeros_like(panel)
    offset = jnp.abs(lax.broadcasted_iota(jnp.int32, (K, SPAN), 1) - WMAX)
    for s in range(ROWS):
        inside = offset <= widths[rows[s]]
        for t in range(TAPS):
            panel[:, pl.ds(0, SPAN)] = jnp.where(inside, basis[rows[s], t], 0.0)
            bands[TAPS * s + t] = pltpu.roll(panel[...], 2 * L - WMAX, 1)

    line = lax.broadcasted_iota(jnp.int32, (L, L), 0)
    lane = lax.broadcasted_iota(jnp.int32, (L, L), 1)

    for s in range(ROWS):
        h, table = HALO[s], tables[s]

        def fill(k, carry, s=s, h=h, table=table):
            for t in range(TAPS):
                band = jnp.broadcast_to(bands[TAPS * s + t, pl.ds(k, 1), :], (L, 2 * L))
                band = pltpu.roll(band, 0, 1, stride=1, stride_axis=0)
                centre, side = band[:, :L], band[:, L:]
                if h == L:
                    to_west = jnp.where(lane < line, side, 0.0)
                    to_east = jnp.where(lane > line, side, 0.0)
                else:
                    to_west, to_east = side[L - h :], side[:h]
                for at, part in ((0, to_west), (h, to_east), (2 * h, centre)):
                    high, low = split(part)
                    size = part.shape[0]
                    table[k, pl.ds(at, size), pl.ds(L * t, L)] = high
                    table[k, pl.ds(at, size), pl.ds(L * (TAPS + t), L)] = low
            return carry

        lax.fori_loop(0, K, fill, 0)

    fetch.wait()

    def weigh(k, carry):
        high, low = split(wf[k])
        wh[:, pl.ds(pl.multiple_of(k * channels, channels), channels)] = high
        wl[:, pl.ds(pl.multiple_of(k * channels, channels), channels)] = low
        return carry

    lax.fori_loop(0, K, weigh, 0)

    own.wait()
    for r in range(ROWS):
        for dst in (r, 2 * ROWS + r):
            send(r, dst, r, east).wait_recv()

    for s in range(ROWS):
        for t in range(TAPS):
            high, low = split(ext[rows[s] + ROWS + taps[rows[s], t]])
            xs[s, :, pl.ds(L * t, L)] = high
            xs[s, :, pl.ds(L * (TAPS + t), L)] = high
            xs[s, :, pl.ds(L * (2 * TAPS + t), L)] = low

    def convolve(s, start, size):
        def correlate(k, carry):
            band = tables[s][k, pl.ds(start, size), :]
            band = jnp.concatenate([band, band[:, : TAPS * L]], axis=1)
            value = lax.dot_general(band, xs[s], NT, preferred_element_type=jnp.float32)
            high, low = split(value)
            place = pl.ds(pl.multiple_of(k * channels, channels), channels)
            ch[pl.ds(0, size), place] = high
            cl[pl.ds(0, size), place] = low
            return carry

        lax.fori_loop(0, K, correlate, 0)
        high, low = ch[pl.ds(0, size), :], cl[pl.ds(0, size), :]
        dot = functools.partial(lax.dot_general, dimension_numbers=NT, preferred_element_type=jnp.float32)
        return dot(high, wh[...]) + dot(high, wl[...]) + dot(low, wh[...])

    def halo(side, s):
        span = pl.ds(BASE[s], HALO[s])
        return pltpu.make_async_remote_copy(
            src_ref=hsend.at[side, span], dst_ref=hrecv.at[side, span], send_sem=hsend_sem.at[side, s],
            recv_sem=hrecv_sem.at[side, s], device_id=(west, east)[side], device_id_type=MESH,
        )

    def hand_over(s, value):
        h = HALO[s]
        for side in range(2):
            hsend[side, pl.ds(BASE[s], h), :] = value[side * h : side * h + h]
            halo(side, s).start()

    hand_over(0, convolve(0, 0, 2 * L))
    for s in range(1, ROWS):
        h = HALO[s]
        value = convolve(s, 0, 2 * h + L)
        hand_over(s, value)
        acc[s] = value[2 * h :]
    acc[0] = convolve(0, 2 * L, L)

    for s in range(ROWS):
        h = HALO[s]
        for side in range(2):
            halo(side, s).wait_recv()
        acc[s, pl.ds(L - h, h), :] += hrecv[0, pl.ds(BASE[s], h), :]
        acc[s, pl.ds(0, h), :] += hrecv[1, pl.ds(BASE[s], h), :]
        out[rows[s]] = jnp.transpose(acc[s] + bias[...])

    for r in range(ROWS):
        send(r, r, r, east).wait_send()
        send(r, r, ROWS + r, east).wait_send()
    for s in range(ROWS):
        for side in range(2):
            halo(side, s).wait_send()


def per_device(lats, lons, features, basis_panels, weights, bias_term, widths, tap_rows):
    channels = features.shape[1]
    bf16, f32 = jnp.bfloat16, jnp.float32
    vmem, smem = pl.BlockSpec(memory_space=pltpu.VMEM), pl.BlockSpec(memory_space=pltpu.SMEM)
    anywhere = pl.BlockSpec(memory_space=pl.ANY)
    return pl.pallas_call(
        functools.partial(kernel, lats, lons),
        out_shape=jax.ShapeDtypeStruct(features.shape, f32),
        in_specs=[smem, smem, vmem, vmem, anywhere, anywhere],
        out_specs=vmem,
        scratch_shapes=[
            pltpu.VMEM((3 * ROWS, channels, L), f32),
            pltpu.VMEM(weights.shape, f32),
            pltpu.VMEM((channels, K * channels), bf16),
            pltpu.VMEM((channels, K * channels), bf16),
            pltpu.VMEM((K, 2 * L), f32),
            pltpu.VMEM((ROWS * TAPS, K, 2 * L), f32),
            *(pltpu.VMEM((K, 2 * h + L, 2 * TAPS * L), bf16) for h in HALO),
            pltpu.VMEM((ROWS, channels, 3 * TAPS * L), bf16),
            pltpu.VMEM((2 * L, K * channels), bf16),
            pltpu.VMEM((2 * L, K * channels), bf16),
            pltpu.VMEM((ROWS, L, channels), f32),
            pltpu.VMEM((2, HALOS, channels), f32),
            pltpu.VMEM((2, HALOS, channels), f32),
            pltpu.SemaphoreType.DMA((2 * ROWS,)),
            pltpu.SemaphoreType.DMA((3 * ROWS,)),
            pltpu.SemaphoreType.DMA((2, ROWS)),
            pltpu.SemaphoreType.DMA((2, ROWS)),
            pltpu.SemaphoreType.DMA,
            pltpu.SemaphoreType.DMA,
        ],
        compiler_params=pltpu.CompilerParams(
            collective_id=0, has_side_effects=True, vmem_limit_bytes=56 << 20
        ),
    )(widths, tap_rows, bias_term[None, :], basis_panels, features, weights)


def solution(mesh):
    return jax.shard_map(
        functools.partial(per_device, mesh.shape["lat"], mesh.shape["lon"]),
        mesh=mesh,
        in_specs=(
            P("lat", None, "lon"),
            P("lat", None, None, None),
            P(),
            P(),
            P("lat"),
            P("lat", None),
        ),
        out_specs=P("lat", None, "lon"),
        check_vma=False,
    )
```

time: 1420 us -> 51.6 us (0.04)
  local copies, waits for them, and re-layouts: 1240 us -> 3.47 us
  waiting for transfers between devices: 78.7 us -> 0 us
  matrix products: 55.1 us -> 0 us
  Pallas kernels: 0 us -> 47.9 us
    gather x12 -> x0, local copies, waits for them, and re-layouts: 1210 us -> none  [the longest x8 1200 us: one_row(): gathered_panel = jnp.take(basis_panels[row_index], clipped, axis=2)]
    ppermute x5 -> x0, waiting for transfers between devices: 78.7 us -> none  [the longest x3 78.7 us: passed_along(): lax.ppermute(value, axis, [(i, (i + by) % peers) for i in range(peers)])]
    dot_general x8 -> x0, matrix products: 55.1 us -> none  [the longest x4 45.2 us: one_row(): jnp.einsum('tcm,tkml->kcl', chosen, toeplitz, precision=lax.Precision.HIG...]
    pallas_call x0 -> x1, Pallas kernels: none -> 47.9 us  [per_device(): pl.pallas_call(functools.partial(kernel, lats, lons), out_shape=jax.Shape...]
  transfers between devices with their start and end apart: 5 -> 0, of which waited for: 3 -> 0; matrix products, arithmetic and copies ran while one was open for 0% -> 0% of each run, Pallas kernels for 0% -> 0%
where the time goes in v1:
time: 51.6 us; the launch traced here: 51.4 us
  Pallas kernels  47.9 us (93%)
  local copies, waits for them, and re-layouts  3.47 us (7%)
    pallas_call x1, Pallas kernels, per_device(): pl.pallas_call(functools.partial(kernel, lats, lons), out_shape=jax.Shape...  47.9 us
    unnamed x2, local copies, waits for them, and re-layouts  3.47 us

profile of v1, /device:TPU:32, one launch (start us, length us, event | category | flops | bytes accessed | tf_op | source)
XLA Modules:
  0.0 51.4 jit_solution(7613410542029949785)
XLA Ops:
  0.0 1.6 %copy.7.basis = f32[4,3,9,255]{3,2,1,0:T(8,128)} copy(f32[4,3,9,255]{3,0,2,1:T(4,128)} %param.7) | data formatting | bytes 220320 | tf_op args[1]
  1.6 47.9 %shard_map.64 = f32[4,256,128]{2,1,0:T(8,128)} custom-call(s32[4]{0:T(128)} %widths.1, s32[4,3]{1,0:T(4,128)} %taps.1, f32[1,256]{1,0:T(1,128)} %bitcast.1, f32[4,3,9,255]{3,2,1,0:T(8,128)} %copy.7.basis, f32[4,256,128]{2,1,0:T(8,128)} %feat.1, f32[9,256,256]{2,1,0:T(8,128)} %weights.1), custom_call_target="tpu_custom_call" | custom-call | tf_op jit(solution)/shard_map/pallas_call | solution.py:218
  49.5 1.9 %copy.9 = f32[4,256,128]{2,1,0:T(8,128)} copy(f32[4,256,128]{2,1,0:T(8,128)} %shard_map.64) | data formatting | bytes 1048576

commit v2 on v1

v2 whole, which is shorter than its diff:
```python
import functools

import jax
import jax.numpy as jnp
from jax import lax
from jax.experimental import pallas as pl
from jax.experimental.pallas import tpu as pltpu
from jax.sharding import PartitionSpec as P

ROWS = 4
TAPS = 3
K = 9
SPAN = 255
WMAX = 127
L = 128
HALO = (128, 48, 48, 32)
GROUP = (0, 1, 1, 1)
BASE = (0, 0, 48, 96)
MESH = pl.DeviceIdType.MESH
NT = (((1,), (1,)), ((), ()))


def split(x):
    high = x.astype(jnp.bfloat16)
    low = (x - high.astype(jnp.float32)).astype(jnp.bfloat16)
    return high, low


def product(a, b):
    return lax.dot_general(a, b, NT, preferred_element_type=jnp.float32)


def kernel(
    lats, lons,
    widths_in, taps_in, bias_in, basis_in, feat, weights,
    out,
    widths, taps, bias, basis, ext, wf, wh, wl, panel, bands, h0, h1, h2, h3, centre, xs, sides, middle, shift, hsend, hrecv,
    send_sem, recv_sem, hsend_sem, hrecv_sem, own_sem, w_sem, small_sem,
):
    la, lo = lax.axis_index("lat"), lax.axis_index("lon")
    channels = ext.shape[1]
    east = {"lat": la, "lon": lax.rem(lo + 1, lons)}
    west = {"lat": la, "lon": lax.rem(lo + lons - 1, lons)}
    half = {"lat": la, "lon": lax.rem(lo + lons // 2, lons)}
    above = {"lat": lax.rem(la + lats - 1, lats), "lon": lo}
    below = {"lat": lax.rem(la + 1, lats), "lon": lo}
    first, last = la == 0, la == lats - 1

    barrier = pltpu.get_barrier_semaphore()

    def greet(peer):
        pl.semaphore_signal(barrier, inc=1, device_id=peer, device_id_type=MESH)

    greet(east)
    greet(west)

    @pl.when(first)
    def _():
        greet(half)

    @pl.when(jnp.logical_not(first))
    def _():
        greet(above)

    @pl.when(last)
    def _():
        greet(half)

    @pl.when(jnp.logical_not(last))
    def _():
        greet(below)

    small = [
        pltpu.make_async_copy(src, dst, small_sem.at[i])
        for i, (src, dst) in enumerate(((widths_in, widths), (taps_in, taps), (bias_in, bias), (basis_in, basis)))
    ]
    own = pltpu.make_async_copy(feat, ext.at[pl.ds(ROWS, ROWS)], own_sem)
    fetch = pltpu.make_async_copy(weights, wf, w_sem)
    for copy in (*small, own, fetch):
        copy.start()
    pl.semaphore_wait(barrier, 4)

    def send(src, dst, place, peer):
        return pltpu.make_async_remote_copy(
            src_ref=feat.at[src], dst_ref=ext.at[dst], send_sem=send_sem.at[place],
            recv_sem=recv_sem.at[dst], device_id=peer, device_id_type=MESH,
        )

    @pl.when(first)
    def _():
        for r in range(ROWS):
            send(r, ROWS - 1 - r, r, half).start()

    @pl.when(last)
    def _():
        for r in range(ROWS):
            send(r, 3 * ROWS - 1 - r, ROWS + r, half).start()

    @pl.when(jnp.logical_not(first))
    def _():
        for r in range(ROWS):
            send(r, 2 * ROWS + r, r, above).start()

    @pl.when(jnp.logical_not(last))
    def _():
        for r in range(ROWS):
            send(r, r, ROWS + r, below).start()

    flip = la // (lats // 2)
    rows = [s + flip * (ROWS - 1 - 2 * s) for s in range(ROWS)]

    for copy in small:
        copy.wait()
    row = lax.broadcasted_iota(jnp.int32, (ROWS, SPAN), 0)
    limit = jnp.full((ROWS, SPAN), widths[0])
    for r in range(1, ROWS):
        limit = jnp.where(row == r, widths[r], limit)
    inside = jnp.abs(lax.broadcasted_iota(jnp.int32, (ROWS, SPAN), 1) - WMAX) <= limit
    panel[...] = jnp.zeros_like(panel)
    for t in range(TAPS):
        for k in range(K):
            panel[K * t + k, :, pl.ds(0, SPAN)] = jnp.where(inside, basis[t, k], 0.0)
            bands[K * t + k] = pltpu.roll(panel[K * t + k], 2 * L - WMAX, 1)

    line = lax.broadcasted_iota(jnp.int32, (L, L), 0)
    lane = lax.broadcasted_iota(jnp.int32, (L, L), 1)
    beside = (h0, h1, h2, h3)

    for s in range(ROWS):

        def fill(k, carry, s=s, h=HALO[s], table=beside[s]):
            for t in range(TAPS):
                band = jnp.broadcast_to(bands[K * t + k, pl.ds(rows[s], 1), :], (L, 2 * L))
                band = pltpu.roll(band, 0, 1, stride=1, stride_axis=0)
                inner, side = band[:, :L], band[:, L:]
                if h == L:
                    to_west = jnp.where(lane < line, side, 0.0)
                    to_east = jnp.where(lane > line, side, 0.0)
                else:
                    to_west, to_east = side[L - h :], side[:h]
                both = jnp.concatenate([to_west, to_east], axis=0)
                spot = pl.ds(pl.multiple_of(k * 2 * h, 2 * h), 2 * h)
                for part, value in enumerate(split(both)):
                    table[spot, pl.ds(L * (TAPS * part + t), L)] = value
                spot = pl.ds(pl.multiple_of(k * L, L), L)
                for part, value in enumerate(split(inner)):
                    centre[s, spot, pl.ds(L * (TAPS * part + t), L)] = value
            return carry

        lax.fori_loop(0, K, fill, 0)

    shift[...] = jnp.transpose(jnp.broadcast_to(bias[...], (L, channels)))
    fetch.wait()

    def weigh(k, carry):
        high, low = split(wf[k])
        wh[:, pl.ds(pl.multiple_of(k * channels, channels), channels)] = high
        wl[:, pl.ds(pl.multiple_of(k * channels, channels), channels)] = low
        return carry

    lax.fori_loop(0, K, weigh, 0)

    own.wait()
    for r in range(ROWS):
        for dst in (r, 2 * ROWS + r):
            send(r, dst, r, east).wait_recv()

    def choose(s):
        for t in range(TAPS):
            high, low = split(ext[rows[s] + ROWS + taps[rows[s], t]])
            xs[s, :, pl.ds(L * t, L)] = high
            xs[s, :, pl.ds(L * (TAPS + t), L)] = high
            xs[s, :, pl.ds(L * (2 * TAPS + t), L)] = low

    def correlate(s, table):
        bands = jnp.concatenate([table[...], table[:, : TAPS * L]], axis=1)
        return split(product(bands, xs[s]))

    def mix(high, low):
        return product(
            jnp.concatenate([wh[...], wh[...], wl[...]], axis=1), jnp.concatenate([high, low, high], axis=1)
        )

    def correlate_sides(s):
        h = HALO[s]
        for part, value in enumerate(correlate(s, beside[s])):
            for k in range(K):
                for side in range(2):
                    sides[part, GROUP[s], pl.ds(L * side + BASE[s], h), pl.ds(channels * k, channels)] = value[
                        (2 * k + side) * h : (2 * k + side + 1) * h
                    ]

    def correlate_centre(s):
        for part, value in enumerate(correlate(s, centre.at[s])):
            for k in range(K):
                middle[part, pl.ds(L * s, L), pl.ds(channels * k, channels)] = value[k * L : (k + 1) * L]

    def halo(side, group):
        return pltpu.make_async_remote_copy(
            src_ref=hsend.at[group, side], dst_ref=hrecv.at[group, side], send_sem=hsend_sem.at[group, side],
            recv_sem=hrecv_sem.at[group, side], device_id=(west, east)[side], device_id_type=MESH,
        )

    def hand_over(group):
        value = mix(sides[0, group], sides[1, group])
        for side in range(2):
            hsend[group, side] = value[:, L * side : L * (side + 1)]
            halo(side, group).start()

    choose(0)
    correlate_sides(0)
    hand_over(0)
    for s in range(1, ROWS):
        choose(s)
        correlate_sides(s)
    hand_over(1)
    for s in range(ROWS):
        correlate_centre(s)
    value = mix(middle[0], middle[1])

    for group in range(2):
        for side in range(2):
            halo(side, group).wait_recv()
    lane = lax.broadcasted_iota(jnp.int32, (channels, L), 1)
    for s in range(ROWS):
        h = HALO[s]
        total = value[:, L * s : L * (s + 1)] + shift[...]
        if h == L:
            total = total + hrecv[0, 0] + hrecv[0, 1]
        else:
            last_columns = pltpu.roll(hrecv[1, 0], L - h - BASE[s], 1)
            first_columns = hrecv[1, 1] if BASE[s] == 0 else pltpu.roll(hrecv[1, 1], L - BASE[s], 1)
            total = total + jnp.where(lane >= L - h, last_columns, 0.0) + jnp.where(lane < h, first_columns, 0.0)
        out[rows[s]] = total

    for r in range(ROWS):
        send(r, r, r, east).wait_send()
        send(r, r, ROWS + r, east).wait_send()
    for group in range(2):
        for side in range(2):
            halo(side, group).wait_send()


def per_device(lats, lons, features, basis_panels, weights, bias_term, widths, tap_rows):
    channels = features.shape[1]
    bf16, f32 = jnp.bfloat16, jnp.float32
    vmem, anywhere = pl.BlockSpec(memory_space=pltpu.VMEM), pl.BlockSpec(memory_space=pl.ANY)
    return pl.pallas_call(
        functools.partial(kernel, lats, lons),
        out_shape=jax.ShapeDtypeStruct(features.shape, f32),
        in_specs=[anywhere] * 6,
        out_specs=vmem,
        scratch_shapes=[
            pltpu.SMEM(widths.shape, jnp.int32),
            pltpu.SMEM(tap_rows.shape, jnp.int32),
            pltpu.VMEM((1, channels), f32),
            pltpu.VMEM((TAPS, K, ROWS, SPAN), f32),
            pltpu.VMEM((3 * ROWS, channels, L), f32),
            pltpu.VMEM(weights.shape, f32),
            pltpu.VMEM((channels, K * channels), bf16),
            pltpu.VMEM((channels, K * channels), bf16),
            pltpu.VMEM((TAPS * K, ROWS, 2 * L), f32),
            pltpu.VMEM((TAPS * K, ROWS, 2 * L), f32),
            *(pltpu.VMEM((K * 2 * h, 2 * TAPS * L), bf16) for h in HALO),
            pltpu.VMEM((ROWS, K * L, 2 * TAPS * L), bf16),
            pltpu.VMEM((ROWS, channels, 3 * TAPS * L), bf16),
            pltpu.VMEM((2, 2, 2 * L, K * channels), bf16),
            pltpu.VMEM((2, ROWS * L, K * channels), bf16),
            pltpu.VMEM((channels, L), f32),
            pltpu.VMEM((2, 2, channels, L), f32),
            pltpu.VMEM((2, 2, channels, L), f32),
            pltpu.SemaphoreType.DMA((2 * ROWS,)),
            pltpu.SemaphoreType.DMA((3 * ROWS,)),
            pltpu.SemaphoreType.DMA((2, 2)),
            pltpu.SemaphoreType.DMA((2, 2)),
            pltpu.SemaphoreType.DMA,
            pltpu.SemaphoreType.DMA,
            pltpu.SemaphoreType.DMA((4,)),
        ],
        compiler_params=pltpu.CompilerParams(
            collective_id=0, has_side_effects=True, vmem_limit_bytes=60 << 20
        ),
    )(widths, tap_rows, bias_term[None, :], jnp.transpose(basis_panels, (1, 2, 0, 3)), features, weights)


def solution(mesh):
    return jax.shard_map(
        functools.partial(per_device, mesh.shape["lat"], mesh.shape["lon"]),
        mesh=mesh,
        in_specs=(
            P("lat", None, "lon"),
            P("lat", None, None, None),
            P(),
            P(),
            P("lat"),
            P("lat", None),
        ),
        out_specs=P("lat", None, "lon"),
        check_vma=False,
    )
```

time: 51.6 us -> 39.6 us (0.77)
  Pallas kernels: 47.9 us -> 37.6 us
  local copies, waits for them, and re-layouts: 3.47 us -> 1.87 us
    pallas_call x1, Pallas kernels: 47.9 us -> 37.6 us  [per_device(): pl.pallas_call(functools.partial(kernel, lats, lons), out_shape=jax.Shape...]
    unnamed x2 -> x1, local copies, waits for them, and re-layouts: 3.47 us -> 1.87 us
where the time goes in v2:
time: 39.6 us; the launch traced here: 39.5 us
  Pallas kernels  37.6 us (95%)
  local copies, waits for them, and re-layouts  1.87 us (5%)
    pallas_call x1, Pallas kernels, per_device(): pl.pallas_call(functools.partial(kernel, lats, lons), out_shape=jax.Shape...  37.6 us
    unnamed x1, local copies, waits for them, and re-layouts  1.87 us

profile of v2, /device:TPU:32, one launch (start us, length us, event | category | flops | bytes accessed | tf_op | source)
XLA Modules:
  0.0 39.5 jit_solution(14877223364267331279)
XLA Ops:
  0.0 37.6 %shard_map.64 = f32[4,256,128]{2,1,0:T(8,128)} custom-call(s32[4]{0:T(128)} %widths_in.1, s32[4,3]{1,0:T(4,128)} %taps_in.1, f32[1,256]{1,0:T(1,128)} %bitcast.3, f32[3,9,4,255]{3,2,1,0:T(4,128)} %bitcast.2, f32[4,256,128]{2,1,0:T(8,128)} %feat.1, f32[9,256,256]{2,1,0:T(8,128)} %weights.1), custom_call_target="tpu_custom_call" | custom-call | tf_op jit(solution)/shard_map/pallas_call | solution.py:248
  37.6 1.9 %copy.8 = f32[4,256,128]{2,1,0:T(8,128)} copy(f32[4,256,128]{2,1,0:T(8,128)} %shard_map.64) | data formatting | bytes 1048576

commit v3 on v2

v3 whole, which is shorter than its diff:
```python
import functools

import jax
import jax.numpy as jnp
from jax import lax
from jax.experimental import pallas as pl
from jax.experimental.pallas import tpu as pltpu
from jax.sharding import PartitionSpec as P

ROWS = 4
TAPS = 3
K = 9
SPAN = 255
WMAX = 127
L = 128
NEAR = (24, 48, 32, 24)
START = (0, 80, 48, 24)
SIDES = 2 * L
CENTRES = 5 * L
WIDE = 9 * L
MESH = pl.DeviceIdType.MESH


def split(x):
    high = x.astype(jnp.bfloat16)
    low = (x - high.astype(jnp.float32)).astype(jnp.bfloat16)
    return high, low


def product(a, b):
    return jnp.dot(a, b, preferred_element_type=jnp.float32)


def kernel(
    lats, lons,
    widths_in, taps_in, bias_in, basis_in, feat, weights,
    out,
    widths, taps, bias, basis, ext0, ext1, wf, wh, wl, panel, bands, t0, t1, t2, t3, xs, cr, acc, shift, hsend, hrecv,
    send_sem, recv_sem, hsend_sem, hrecv_sem, own_sem, w_sem, small_sem,
):
    la, lo = lax.axis_index("lat"), lax.axis_index("lon")
    channels, ext = feat.shape[1], (ext0, ext1)
    east = {"lat": la, "lon": lax.rem(lo + 1, lons)}
    west = {"lat": la, "lon": lax.rem(lo + lons - 1, lons)}
    half = {"lat": la, "lon": lax.rem(lo + lons // 2, lons)}
    above = {"lat": lax.rem(la + lats - 1, lats), "lon": lo}
    below = {"lat": lax.rem(la + 1, lats), "lon": lo}
    first, last = la == 0, la == lats - 1

    barrier = pltpu.get_barrier_semaphore()

    def greet(peer):
        pl.semaphore_signal(barrier, inc=1, device_id=peer, device_id_type=MESH)

    greet(east)
    greet(west)

    @pl.when(first)
    def _():
        greet(half)

    @pl.when(jnp.logical_not(first))
    def _():
        greet(above)

    @pl.when(last)
    def _():
        greet(half)

    @pl.when(jnp.logical_not(last))
    def _():
        greet(below)

    small = [
        pltpu.make_async_copy(src, dst, small_sem.at[i])
        for i, (src, dst) in enumerate(((widths_in, widths), (taps_in, taps), (bias_in, bias), (basis_in, basis)))
    ]
    part = channels // 2
    own = [
        pltpu.make_async_copy(feat.at[:, pl.ds(part * q, part)], ext[q].at[pl.ds(ROWS, ROWS)], own_sem.at[q])
        for q in range(2)
    ]
    fetch = pltpu.make_async_copy(weights, wf, w_sem)
    for copy in (*small, *own, fetch):
        copy.start()
    pl.semaphore_wait(barrier, 4)

    def send(src, dst, q, place, peer):
        some = pl.ds(part * q, part)
        return pltpu.make_async_remote_copy(
            src_ref=feat.at[src, some], dst_ref=ext[q].at[dst], send_sem=send_sem.at[q, place],
            recv_sem=recv_sem.at[q, dst], device_id=peer, device_id_type=MESH,
        )

    for q in range(2):

        @pl.when(first)
        def _(q=q):
            for r in range(ROWS):
                send(r, ROWS - 1 - r, q, r, half).start()

        @pl.when(last)
        def _(q=q):
            for r in range(ROWS):
                send(r, 3 * ROWS - 1 - r, q, ROWS + r, half).start()

        @pl.when(jnp.logical_not(first))
        def _(q=q):
            for r in range(ROWS):
                send(r, 2 * ROWS + r, q, r, above).start()

        @pl.when(jnp.logical_not(last))
        def _(q=q):
            for r in range(ROWS):
                send(r, r, q, ROWS + r, below).start()

    flip = la // (lats // 2)
    rows = [s + flip * (ROWS - 1 - 2 * s) for s in range(ROWS)]

    for copy in small:
        copy.wait()
    row = lax.broadcasted_iota(jnp.int32, (ROWS, SPAN), 0)
    limit = jnp.full((ROWS, SPAN), widths[0])
    for r in range(1, ROWS):
        limit = jnp.where(row == r, widths[r], limit)
    inside = jnp.abs(lax.broadcasted_iota(jnp.int32, (ROWS, SPAN), 1) - WMAX) <= limit
    panel[...] = jnp.zeros_like(panel)
    for t in range(TAPS):
        for k in range(K):
            panel[pl.ds(ROWS * (K * t + k), ROWS), pl.ds(0, SPAN)] = jnp.where(inside, basis[t, k], 0.0)
    source = lax.broadcasted_iota(jnp.int32, (2 * L, 2 * L), 0)
    target = lax.broadcasted_iota(jnp.int32, (2 * L, 2 * L), 1)
    back = WMAX - target
    back = jnp.where(back < -1, back + 2 * L, back)
    move = jnp.where(source == back, 1.0, 0.0).astype(jnp.bfloat16)
    high, low = split(panel[...])
    bands[...] = product(high, move) + product(low, move)

    line = lax.broadcasted_iota(jnp.int32, (L, L), 0)
    lane = lax.broadcasted_iota(jnp.int32, (L, L), 1)
    tables = (t0, t1, t2, t3)
    outer = [2 * L, L, L, L]

    for s in range(ROWS):

        def fill(k, carry, s=s, table=tables[s], width=outer[s]):
            for t in range(TAPS):
                band = jnp.broadcast_to(bands[pl.ds(ROWS * (K * t + k) + rows[s], 1), :], (L, 2 * L))
                band = pltpu.roll(band, 0, 1, stride=1, stride_axis=0)
                inner, side = band[:, :L], band[:, L:]
                if width == 2 * L:
                    side = jnp.concatenate(
                        [jnp.where(line < lane, side, 0.0), jnp.where(line > lane, side, 0.0)], axis=1
                    )
                for at, value in ((k * width, side), (K * width + k * L, inner)):
                    spot = pl.ds(pl.multiple_of(at, L), value.shape[1])
                    for p, piece in enumerate(split(value)):
                        table[pl.ds(L * (TAPS * p + t), L), spot] = piece
            return carry

        lax.fori_loop(0, K, fill, 0)

    shift[...] = jnp.transpose(jnp.broadcast_to(bias[...], (L, channels)))
    fetch.wait()

    def weigh(k, carry):
        spot = pl.ds(pl.multiple_of(k * part, part), part)
        high, low = split(wf[k])
        for q in range(2):
            wh[q, :, spot] = high[:, part * q : part * (q + 1)]
            wl[q, :, spot] = low[:, part * q : part * (q + 1)]
        return carry

    lax.fori_loop(0, K, weigh, 0)
    for copy in own:
        copy.wait()

    def choose(q, s):
        for t in range(TAPS):
            high, low = split(ext[q][rows[s] + ROWS + taps[rows[s], t]])
            xs[q, s, :, pl.ds(L * t, L)] = high
            xs[q, s, :, pl.ds(L * (TAPS + t), L)] = high
            xs[q, s, :, pl.ds(L * (2 * TAPS + t), L)] = low

    def correlate(q, s, start, width, at):
        size = K * width
        table = tables[s]
        bands = jnp.concatenate([table[:, start : start + size], table[: TAPS * L, start : start + size]], axis=0)
        for p, value in enumerate(split(product(xs[q, s], bands))):
            for k in range(K):
                cr[p, q, pl.ds(part * k, part), pl.ds(at, width)] = value[:, width * k : width * (k + 1)]

    def correlate_sides(q, s):
        correlate(q, s, 0, outer[s], 0 if s == 0 else SIDES + L * (s - 1))

    def correlate_centre(q, s):
        correlate(q, s, K * outer[s], L, CENTRES + L * s)

    def mix(q, start, stop):
        high, low = cr[0, q, :, start:stop], cr[1, q, :, start:stop]
        return product(
            jnp.concatenate([wh[q], wh[q], wl[q]], axis=1), jnp.concatenate([high, low, high], axis=0)
        )

    def halo(side, group):
        return pltpu.make_async_remote_copy(
            src_ref=hsend.at[group, side], dst_ref=hrecv.at[group, side], send_sem=hsend_sem.at[group, side],
            recv_sem=hrecv_sem.at[group, side], device_id=(west, east)[side], device_id_type=MESH,
        )

    def arrive(q):
        for r in range(ROWS):
            for dst in (r, 2 * ROWS + r):
                send(r, dst, q, r, east).wait_recv()

    arrive(0)
    for s in range(ROWS):
        choose(0, s)
        correlate_sides(0, s)
        correlate_centre(0, s)
    acc[...] = mix(0, 0, WIDE)

    arrive(1)
    pole = jnp.logical_or(first, last)
    choose(1, 0)
    correlate_sides(1, 0)
    wide = mix(1, 0, SIDES) + acc[:, :SIDES]
    hsend[0, 0] = wide[:, :L]
    hsend[0, 1] = wide[:, L:]

    @pl.when(pole)
    def _():
        for side in range(2):
            halo(side, 0).start()

    for s in range(1, ROWS):
        choose(1, s)
        correlate_sides(1, s)
    value = mix(1, SIDES, CENTRES) + acc[:, SIDES:CENTRES]
    lane = lax.broadcasted_iota(jnp.int32, (channels, L), 1)
    for side in range(2):
        packed = jnp.zeros((channels, L), jnp.float32)
        for s in range(ROWS):
            block = hsend[0, side] if s == 0 else value[:, L * (s - 1) : L * s]
            by = (START[s] - (L - NEAR[s] if side == 0 else 0)) % L
            block = pltpu.roll(block, by, 1) if by else block
            packed = jnp.where((lane >= START[s]) & (lane < START[s] + NEAR[s]), block, packed)
        hsend[1, side] = packed
        halo(side, 1).start()
    for s in range(ROWS):
        correlate_centre(1, s)
    value = mix(1, CENTRES, WIDE) + acc[:, CENTRES:]

    @pl.when(pole)
    def _():
        for side in range(2):
            halo(side, 0).wait_recv()

    for side in range(2):
        halo(side, 1).wait_recv()
    for s in range(ROWS):
        total = value[:, L * s : L * (s + 1)] + shift[...]
        for side in range(2):
            by = ((L - NEAR[s] if side == 0 else 0) - START[s]) % L
            block = pltpu.roll(hrecv[1, side], by, 1) if by else hrecv[1, side]
            near = (lane >= L - NEAR[s]) if side == 0 else (lane < NEAR[s])
            total = total + jnp.where(near, block, 0.0)
            if s == 0:
                total = total + jnp.where(jnp.logical_and(pole, jnp.logical_not(near)), hrecv[0, side], 0.0)
        out[rows[s]] = total

    for q in range(2):
        for r in range(ROWS):
            send(r, r, q, r, east).wait_send()
            send(r, r, q, ROWS + r, east).wait_send()

    @pl.when(pole)
    def _():
        for side in range(2):
            halo(side, 0).wait_send()

    for side in range(2):
        halo(side, 1).wait_send()


def per_device(lats, lons, features, basis_panels, weights, bias_term, widths, tap_rows):
    channels = features.shape[1]
    bf16, f32 = jnp.bfloat16, jnp.float32
    vmem, anywhere = pl.BlockSpec(memory_space=pltpu.VMEM), pl.BlockSpec(memory_space=pl.ANY)
    return pl.pallas_call(
        functools.partial(kernel, lats, lons),
        out_shape=jax.ShapeDtypeStruct(features.shape, f32),
        in_specs=[anywhere] * 6,
        out_specs=vmem,
        scratch_shapes=[
            pltpu.SMEM(widths.shape, jnp.int32),
            pltpu.SMEM(tap_rows.shape, jnp.int32),
            pltpu.VMEM((1, channels), f32),
            pltpu.VMEM((TAPS, K, ROWS, SPAN), f32),
            pltpu.VMEM((3 * ROWS, channels // 2, L), f32),
            pltpu.VMEM((3 * ROWS, channels // 2, L), f32),
            pltpu.VMEM(weights.shape, f32),
            pltpu.VMEM((2, channels, K * channels // 2), bf16),
            pltpu.VMEM((2, channels, K * channels // 2), bf16),
            pltpu.VMEM((TAPS * K * ROWS, 2 * L), f32),
            pltpu.VMEM((TAPS * K * ROWS, 2 * L), f32),
            *(pltpu.VMEM((2 * TAPS * L, K * n * L), bf16) for n in (3, 2, 2, 2)),
            pltpu.VMEM((2, ROWS, channels // 2, 3 * TAPS * L), bf16),
            pltpu.VMEM((2, 2, K * channels // 2, WIDE), bf16),
            pltpu.VMEM((channels, WIDE), f32),
            pltpu.VMEM((channels, L), f32),
            pltpu.VMEM((2, 2, channels, L), f32),
            pltpu.VMEM((2, 2, channels, L), f32),
            pltpu.SemaphoreType.DMA((2, 2 * ROWS)),
            pltpu.SemaphoreType.DMA((2, 3 * ROWS)),
            pltpu.SemaphoreType.DMA((2, 2)),
            pltpu.SemaphoreType.DMA((2, 2)),
            pltpu.SemaphoreType.DMA((2,)),
            pltpu.SemaphoreType.DMA,
            pltpu.SemaphoreType.DMA((4,)),
        ],
        compiler_params=pltpu.CompilerParams(
            collective_id=0, has_side_effects=True, vmem_limit_bytes=60 << 20
        ),
    )(widths, tap_rows, bias_term[None, :], jnp.transpose(basis_panels, (1, 2, 0, 3)), features, weights)


def solution(mesh):
    return jax.shard_map(
        functools.partial(per_device, mesh.shape["lat"], mesh.shape["lon"]),
        mesh=mesh,
        in_specs=(
            P("lat", None, "lon"),
            P("lat", None, None, None),
            P(),
            P(),
            P("lat"),
            P("lat", None),
        ),
        out_specs=P("lat", None, "lon"),
        check_vma=False,
    )
```

time: 39.6 us -> 37.7 us (0.952)
  the two profiles are of different devices: /device:TPU:32 before, /device:TPU:56 now
where the time goes in v3:
time: 37.7 us; the launch traced here: 37.6 us
  Pallas kernels  35.7 us (95%)
  local copies, waits for them, and re-layouts  1.87 us (5%)
    pallas_call x1, Pallas kernels, per_device(): pl.pallas_call(functools.partial(kernel, lats, lons), out_shape=jax.Shape...  35.7 us
    unnamed x1, local copies, waits for them, and re-layouts  1.87 us

profile of v3, /device:TPU:56, one launch (start us, length us, event | category | flops | bytes accessed | tf_op | source)
XLA Modules:
  0.0 37.6 jit_solution(1272559237229816549)
XLA Ops:
  0.0 35.7 %shard_map.64 = f32[4,256,128]{2,1,0:T(8,128)} custom-call(s32[4]{0:T(128)} %widths_in.1, s32[4,3]{1,0:T(4,128)} %taps_in.1, f32[1,256]{1,0:T(1,128)} %bitcast.3, f32[3,9,4,255]{3,2,1,0:T(4,128)} %bitcast.2, f32[4,256,128]{2,1,0:T(8,128)} %feat.1, f32[9,256,256]{2,1,0:T(8,128)} %weights.1), custom_call_target="tpu_custom_call" | custom-call | tf_op jit(solution)/shard_map/pallas_call | solution.py:290
  35.7 1.9 %copy.8 = f32[4,256,128]{2,1,0:T(8,128)} copy(f32[4,256,128]{2,1,0:T(8,128)} %shard_map.64) | data formatting | bytes 1048576

commit v4 on v3

--- a/solution.py
+++ b/solution.py
@@ -18,6 +18,7 @@
 SIDES = 2 * L
 CENTRES = 5 * L
 WIDE = 9 * L
+EARLY = 2
 MESH = pl.DeviceIdType.MESH
 
 
@@ -217,8 +218,9 @@
     for s in range(ROWS):
         choose(0, s)
         correlate_sides(0, s)
+    acc[...] = mix(0, 0, CENTRES)
+    for s in range(EARLY):
         correlate_centre(0, s)
-    acc[...] = mix(0, 0, WIDE)
 
     arrive(1)
     pole = jnp.logical_or(first, last)
@@ -236,7 +238,7 @@
     for s in range(1, ROWS):
         choose(1, s)
         correlate_sides(1, s)
-    value = mix(1, SIDES, CENTRES) + acc[:, SIDES:CENTRES]
+    value = mix(1, SIDES, CENTRES) + acc[:, SIDES:]
     lane = lax.broadcasted_iota(jnp.int32, (channels, L), 1)
     for side in range(2):
         packed = jnp.zeros((channels, L), jnp.float32)
@@ -248,8 +250,10 @@
         hsend[1, side] = packed
         halo(side, 1).start()
     for s in range(ROWS):
+        if s >= EARLY:
+            correlate_centre(0, s)
         correlate_centre(1, s)
-    value = mix(1, CENTRES, WIDE) + acc[:, CENTRES:]
+    value = mix(0, CENTRES, WIDE) + mix(1, CENTRES, WIDE)
 
     @pl.when(pole)
     def _():
@@ -307,7 +311,7 @@
             *(pltpu.VMEM((2 * TAPS * L, K * n * L), bf16) for n in (3, 2, 2, 2)),
             pltpu.VMEM((2, ROWS, channels // 2, 3 * TAPS * L), bf16),
             pltpu.VMEM((2, 2, K * channels // 2, WIDE), bf16),
-            pltpu.VMEM((channels, WIDE), f32),
+            pltpu.VMEM((channels, CENTRES), f32),
             pltpu.VMEM((channels, L), f32),
             pltpu.VMEM((2, 2, channels, L), f32),
             pltpu.VMEM((2, 2, channels, L), f32),

time: 37.7 us -> 36.1 us (0.958)
  the two profiles are of different devices: /device:TPU:56 before, /device:TPU:32 now
where the time goes in v4:
time: 36.1 us; the launch traced here: 35.9 us
  Pallas kernels  34 us (94%)
  local copies, waits for them, and re-layouts  1.87 us (5%)
    pallas_call x1, Pallas kernels, per_device(): pl.pallas_call(functools.partial(kernel, lats, lons), out_shape=jax.Shape...  34 us
    unnamed x1, local copies, waits for them, and re-layouts  1.87 us

profile of v4, /device:TPU:32, one launch (start us, length us, event | category | flops | bytes accessed | tf_op | source)
XLA Modules:
  0.0 35.9 jit_solution(14143851519120648609)
XLA Ops:
  0.0 34.0 %shard_map.64 = f32[4,256,128]{2,1,0:T(8,128)} custom-call(s32[4]{0:T(128)} %widths_in.1, s32[4,3]{1,0:T(4,128)} %taps_in.1, f32[1,256]{1,0:T(1,128)} %bitcast.3, f32[3,9,4,255]{3,2,1,0:T(4,128)} %bitcast.2, f32[4,256,128]{2,1,0:T(8,128)} %feat.1, f32[9,256,256]{2,1,0:T(8,128)} %weights.1), custom_call_target="tpu_custom_call" | custom-call | tf_op jit(solution)/shard_map/pallas_call | solution.py:294
  34.0 1.9 %copy.8 = f32[4,256,128]{2,1,0:T(8,128)} copy(f32[4,256,128]{2,1,0:T(8,128)} %shard_map.64) | data formatting | bytes 1048576

commit v5 on v4

--- a/solution.py
+++ b/solution.py
@@ -293,7 +293,7 @@
     vmem, anywhere = pl.BlockSpec(memory_space=pltpu.VMEM), pl.BlockSpec(memory_space=pl.ANY)
     return pl.pallas_call(
         functools.partial(kernel, lats, lons),
-        out_shape=jax.ShapeDtypeStruct(features.shape, f32),
+        out_shape=pltpu.VMEM(features.shape, f32),
         in_specs=[anywhere] * 6,
         out_specs=vmem,
         scratch_shapes=[

time: 36.1 us -> 34.2 us (0.947)
  local copies, waits for them, and re-layouts: 1.87 us -> 0.8 us
  Pallas kernels: 34 us -> 33.2 us
    unnamed x1, local copies, waits for them, and re-layouts: 1.87 us -> 0.8 us
    pallas_call x1, Pallas kernels: 34 us -> 33.2 us  [per_device(): pl.pallas_call(functools.partial(kernel, lats, lons), out_shape=pltpu.VME...]
where the time goes in v5:
time: 34.2 us; the launch traced here: 34 us
  Pallas kernels  33.2 us (97%)
  local copies, waits for them, and re-layouts  0.8 us (2%)
    pallas_call x1, Pallas kernels, per_device(): pl.pallas_call(functools.partial(kernel, lats, lons), out_shape=pltpu.VME...  33.2 us
    unnamed x1, local copies, waits for them, and re-layouts  0.8 us

profile of v5, /device:TPU:32, one launch (start us, length us, event | category | flops | bytes accessed | tf_op | source)
XLA Modules:
  0.0 34.0 jit_solution(17269759005040698829)
XLA Ops:
  0.0 33.2 %shard_map.64 = f32[4,256,128]{2,1,0:T(8,128)S(1)} custom-call(s32[4]{0:T(128)} %widths_in.1, s32[4,3]{1,0:T(4,128)} %taps_in.1, f32[1,256]{1,0:T(1,128)} %bitcast.3, f32[3,9,4,255]{3,2,1,0:T(4,128)} %bitcast.2, f32[4,256,128]{2,1,0:T(8,128)} %feat.1, f32[9,256,256]{2,1,0:T(8,128)} %weights.1), custom_call_target="tpu_custom_call" | custom-call | tf_op jit(solution)/shard_map/pallas_call | solution.py:294
  33.2 0.8 %copy.8 = f32[4,256,128]{2,1,0:T(8,128)} copy(f32[4,256,128]{2,1,0:T(8,128)S(1)} %shard_map.64) | data formatting | bytes 1048576
